TPU v7x, 512 devices: a whole 4x8x8 slice. The times are simulated.
512 devices in a mesh: tm: 16 (over z_lo, x, core), height: 32 (over y, z_hi).
Axes of the slice: x: 4, y: 8, z: 8 (z_hi: 4, z_lo: 2; z = z_hi * 2 + z_lo), core: 2. Of those that a mesh axis runs over, the one named last changes fastest.
Arguments:
- video_q: bfloat16 [16, 32, 768, 256], P('tm', 'height'), may hold values from -4.5 to 4.5
- video_k: bfloat16 [16, 32, 768, 256], P('tm', 'height'), may hold values from -4.5 to 4.5
- video_v: bfloat16 [16, 32, 768, 256], P('tm', 'height'), may hold values from -6 to 6
- text_k: bfloat16 [256, 256], P('height'), may hold values from -4.5 to 4.5
- text_v: bfloat16 [256, 256], P('height'), may hold values from -6 to 6
- text_valid: int32 [256], replicated, may hold values from 0 to 1, as said below
- extent: int32 [2, 3], replicated, may hold values from 0 to 1
Outputs:
- video_out: bfloat16 [16, 32, 768, 256], P('tm', 'height')
Inputs may be any that keep to these rules, and one draw needn't show every extreme that they name: `text_valid`: the valid text tokens come first; at least 64 are valid and at least one is not.
All inputs are finite; a program needn't handle non-finite values.
Results may differ from a plain program's by a relative error of at most 0.0042.
Values may be sent and summed in bfloat16 or wider, within the bound.
No kernel may reach another device: no remote copies, remote signals or barrier semaphores. Data moves between devices by JAX's collectives and lax.ppermute only.
A program may use at most 64 MiB of HBM per device.

v0:
```python
import math
import jax
import jax.numpy as jnp
from jax import lax
from jax.sharding import PartitionSpec as P

TILE = 384


def padded_2(array, sides, width):
    for axis, dim in sides:
        size, length = (lax.axis_size(axis), array.shape[dim])
        up = [(i, (i + 1) % size) for i in range(size - 1)]
        down = [(j, i) for i, j in up]
        last = lax.slice_in_dim(array, length - width, length, axis=dim)
        initial = lax.slice_in_dim(array, 0, width, axis=dim)
        before = lax.ppermute(last, axis, up)
        after = lax.ppermute(initial, axis, down)
        array = jnp.concatenate([before, array, after], axis=dim)
    return array


def shards(video_q, video_k, video_v, text_k, text_v, text_valid, extent):
    row_count = video_q.shape[2]
    feat_count = video_q.shape[3]
    head_count = extent.shape[0]
    head_width = feat_count // head_count
    tile_count = row_count // TILE
    score_scale = 1.0 / math.sqrt(head_width)
    key_value = jnp.concatenate((video_k, video_v), axis=3)
    padded = padded_2(key_value, (("tm", 0), ("height", 1)), 1)
    slab_all = padded.reshape(9 * row_count, 2 * feat_count)
    text_keys, text_values = (
        lax.all_gather(text_k, "height", axis=0, tiled=True),
        lax.all_gather(text_v, "height", axis=0, tiled=True),
    )
    time_count = lax.axis_size("tm")
    height_count = lax.axis_size("height")
    local_time = lax.axis_index("tm")
    local_height = lax.axis_index("height")
    key_ids = jnp.arange(9 * row_count, dtype=jnp.int32)
    slab_index = key_ids // row_count
    time_gap = slab_index // 3 - 1
    height_gap = slab_index % 3 - 1
    key_tile = key_ids % row_count // TILE
    inside_keys = (local_time + time_gap >= 0) & (local_time + time_gap < time_count)
    inside_keys = (
        inside_keys & (local_height + height_gap >= 0) & (local_height + height_gap < height_count)
    )
    text_ok = text_valid > 0
    queries = video_q[0, 0].reshape(tile_count, TILE, feat_count)

    def one_block(operands):
        query_block, query_tile = operands
        width_gap = jnp.abs(key_tile - query_tile)
        head_outputs = []
        for head_index in range(head_count):
            low = head_index * head_width
            high = low + head_width
            allowed = (
                inside_keys
                & (jnp.abs(time_gap) <= extent[head_index, 0])
                & (jnp.abs(height_gap) <= extent[head_index, 1])
            )
            allowed = allowed & (width_gap <= extent[head_index, 2])
            query_head = query_block[:, low:high]
            video_scores = (
                jnp.einsum(
                    "qd,kd->qk",
                    query_head,
                    slab_all[:, low:high],
                    preferred_element_type=jnp.float32,
                )
                * score_scale
            )
            text_scores = (
                jnp.einsum(
                    "qd,kd->qk",
                    query_head,
                    text_keys[:, low:high],
                    preferred_element_type=jnp.float32,
                )
                * score_scale
            )
            video_scores = jnp.where(allowed[None, :], video_scores, -jnp.inf)
            text_scores = jnp.where(text_ok[None, :], text_scores, -jnp.inf)
            row_top = jnp.maximum(jnp.max(video_scores, axis=1), jnp.max(text_scores, axis=1))
            video_expo = jnp.exp(video_scores - row_top[:, None])
            text_expo = jnp.exp(text_scores - row_top[:, None])
            row_total = jnp.sum(video_expo, axis=1) + jnp.sum(text_expo, axis=1)
            value_low = feat_count + low
            weighted = jnp.dot(
                video_expo.astype(jnp.bfloat16),
                slab_all[:, value_low : value_low + head_width],
                preferred_element_type=jnp.float32,
            )
            weighted = weighted + jnp.dot(
                text_expo.astype(jnp.bfloat16),
                text_values[:, low:high],
                preferred_element_type=jnp.float32,
            )
            head_outputs.append(weighted / row_total[:, None])
        return jnp.concatenate(head_outputs, axis=1).astype(jnp.bfloat16)

    blocks = lax.map(one_block, (queries, jnp.arange(tile_count, dtype=jnp.int32)))
    return blocks.reshape(video_q.shape)


def solution(mesh):
    return jax.shard_map(
        shards,
        mesh=mesh,
        in_specs=(
            P("tm", "height", None, None),
            P("tm", "height", None, None),
            P("tm", "height", None, None),
            P("height", None),
            P("height", None),
            P(),
            P(),
        ),
        out_specs=P("tm", "height", None, None),
        check_vma=False,
    )
```

profile of v0, /device:TPU:4, one launch (start us, length us, event | category | flops | bytes accessed | tf_op | source)
XLA Modules:
  0.0 332.3 jit_solution(4440091307780463444)
XLA Ops:
  0.0 1.0 constant_dynamic-update-slice_fusion.2
  1.0 1.0 constant_dynamic-update-slice_fusion.1
  2.1 1.9 collective-permute-start
  4.0 3.6 %collective-permute-start.1 = (bf16[1,1,768,512]{3,2,1,0:T(8,128)(2,1)S(1)}, bf16[1,1,768,512]{3,2,1,0:T(8,128)(2,1)S(1)}, u32[]{:S(2)}, u32[]{:S(2)}) collective-permute-start(bf16[1,1,768,512]{3,2,1,0:T(8,128)(2,1)S(1)} %constant_dynamic-update-slice_fusion.1), channel_id=1, source_target_pairs={{32,0},{64,32},{96,64},{128,96},{160,128},{192,160},{224,192},{256... | collective-permute-start | bytes 2359304 | tf_op jit(solution)/shard_map/ppermute | solution.py:18
  7.6 7.7 %collective-permute-done = bf16[1,1,768,512]{3,2,1,0:T(8,128)(2,1)S(1)} collective-permute-done((bf16[1,1,768,512]{3,2,1,0:T(8,128)(2,1)S(1)}, bf16[1,1,768,512]{3,2,1,0:T(8,128)(2,1)S(1)}, u32[]{:S(2)}, u32[]{:S(2)}) %collective-permute-start) | collective-permute-done | bytes 786464 | tf_op jit(solution)/shard_map/ppermute | solution.py:17
  15.4 1.8 collective-permute-done.1
  17.1 1.7 pad_maximum_fusion.2
  18.8 7.5 %collective-permute-start.2 = (bf16[3,1,768,512]{3,2,1,0:T(8,128)(2,1)}, bf16[3,1,768,512]{3,2,1,0:T(8,128)(2,1)}, u32[]{:S(2)}, u32[]{:S(2)}) collective-permute-start(bf16[3,1,768,512]{3,2,1,0:T(8,128)(2,1)} %pad_maximum_fusion.2), channel_id=1, source_target_pairs={{0,1},{1,2},{2,3},{3,4},{4,5},{5,6},{6,7},{7,8},{8,9},{9,10},{10,1... | collective-permute-start | bytes 7077896 | tf_op jit(solution)/shard_map/ppermute | solution.py:17
  26.3 1.3 collective-permute-start.3
  27.6 179.9 %all_gather.6 = bf16[256,256]{1,0:T(8,128)(2,1)S(1)} all-gather(bf16[8,256]{1,0:T(8,128)(2,1)} %param.12), channel_id=1, replica_groups=mesh['tm'=16,'height'=32] {'height'}, dimensions={0}, use_global_device_ids=true | all-gather | bytes 135168 | tf_op jit(solution)/shard_map/all_gather | solution.py:34
  207.5 76.3 %all_gather.7 = bf16[256,256]{1,0:T(8,128)(2,1)S(1)} all-gather(bf16[8,256]{1,0:T(8,128)(2,1)} %param.13), channel_id=1, replica_groups=mesh['tm'=16,'height'=32] {'height'}, dimensions={0}, use_global_device_ids=true | all-gather | bytes 135168 | tf_op jit(solution)/shard_map/all_gather | solution.py:35
  283.7 0.7 broadcast_compare_fusion
  284.4 5.9 %pad_maximum_fusion.1 = bf16[3,3,768,512]{3,2,1,0:T(8,128)(2,1)} fusion(bf16[3,1,768,512]{3,2,1,0:T(8,128)(2,1)} %collective-permute-done.3, bf16[1,1,768,512]{3,2,1,0:T(8,128)(2,1)S(1)} %collective-permute-done.1, bf16[1,1,768,512]{3,2,1,0:T(8,128)(2,1)S(1)} %constant_dynamic-update-slice_fusion.1, bf16[1,1,768,512]{3,2,1,0:T(8,128)(2,1)S(1)} %collective-permute-done, ...), kind=kLoop, calls=%fused_computation.95 | loop fusion | flops 14155776 | bytes 14155776 | tf_op jit(solution)/shard_map/concatenate | solution.py:19
  290.3 41.2 %while.15 = (s32[]{:T(128)}, bf16[2,384,256]{2,1,0:T(8,128)(2,1)S(1)}, s32[2,3]{1,0:T(2,128)S(1)}, s32[2]{0:T(128)S(1)}, bf16[2,384,256]{2,1,0:T(8,128)(2,1)S(1)...) while((s32[]{:T(128)}, ...), condition=%wide.region_9.10_spmd.clone.clone, body=%wide.region_0.9_spmd.clone.clone.sunk | while | flops 2858657792 | bytes 97717000 | solution.py:105
  290.3 0.7 fusion.102
  291.0 0.9 compare_reduce_fusion.10
  292.0 1.0 compare_reduce_fusion.11
  292.9 0.8 compare_reduce_fusion.8
  293.8 1.0 compare_reduce_fusion.9
  294.8 0.6 dynamic_slice.22
  295.3 1.9 compare_and_fusion.4
  297.3 3.3 fusion.109
  300.6 0.2 fusion.110
  300.8 1.6 fusion.112
  302.6 2.0 fusion.111
  304.6 0.2 fusion.114
  304.8 1.7 fusion.103
  306.5 0.2 fusion.104
  306.9 1.6 fusion.106
  308.5 2.0 fusion.105
  310.5 0.2 fusion.108
  311.0 0.7 fusion.102
  311.6 0.9 compare_reduce_fusion.10
  312.6 1.0 compare_reduce_fusion.11
  313.6 0.8 compare_reduce_fusion.8
  314.4 1.0 compare_reduce_fusion.9
  315.4 0.6 dynamic_slice.22
  316.0 1.9 compare_and_fusion.4
  317.9 3.3 fusion.109
  321.2 0.2 fusion.110
  321.5 1.6 fusion.112
  323.2 2.0 fusion.111
  325.2 0.2 fusion.114
  325.5 1.7 fusion.103
  327.1 0.2 fusion.104
  327.5 1.6 fusion.106
  329.1 2.0 fusion.105
  331.6 0.7 copy-done.2
  (40 shorter events, 1.1 us)
Async XLA Ops:
  2.1 13.3 %collective-permute-start = (bf16[1,1,768,512]{3,2,1,0:T(8,128)(2,1)S(1)}, bf16[1,1,768,512]{3,2,1,0:T(8,128)(2,1)S(1)}, u32[]{:S(2)}, u32[]{:S(2)}) collective-permute-start(bf16[1,1,768,512]{3,2,1,0:T(8,128)(2,1)S(1)} %constant_dynamic-update-slice_fusion.1), channel_id=1, source_target_pairs={{0,32},{32,64},{64,96},{96,128},{128,160},{160,192},{192,224},{224... | collective-permute-start | bytes 2359304 | tf_op jit(solution)/shard_map/ppermute | solution.py:17
  4.0 13.1 %collective-permute-start.1 = (bf16[1,1,768,512]{3,2,1,0:T(8,128)(2,1)S(1)}, bf16[1,1,768,512]{3,2,1,0:T(8,128)(2,1)S(1)}, u32[]{:S(2)}, u32[]{:S(2)}) collective-permute-start(bf16[1,1,768,512]{3,2,1,0:T(8,128)(2,1)S(1)} %constant_dynamic-update-slice_fusion.1), channel_id=1, source_target_pairs={{32,0},{64,32},{96,64},{128,96},{160,128},{192,160},{224,192},{256... | collective-permute-start | bytes 2359304 | tf_op jit(solution)/shard_map/ppermute | solution.py:18
  18.8 265.6 %collective-permute-start.2 = (bf16[3,1,768,512]{3,2,1,0:T(8,128)(2,1)}, bf16[3,1,768,512]{3,2,1,0:T(8,128)(2,1)}, u32[]{:S(2)}, u32[]{:S(2)}) collective-permute-start(bf16[3,1,768,512]{3,2,1,0:T(8,128)(2,1)} %pad_maximum_fusion.2), channel_id=1, source_target_pairs={{0,1},{1,2},{2,3},{3,4},{4,5},{5,6},{6,7},{7,8},{8,9},{9,10},{10,1... | collective-permute-start | bytes 7077896 | tf_op jit(solution)/shard_map/ppermute | solution.py:17
  26.3 258.2 %collective-permute-start.3 = (bf16[3,1,768,512]{3,2,1,0:T(8,128)(2,1)}, bf16[3,1,768,512]{3,2,1,0:T(8,128)(2,1)}, u32[]{:S(2)}, u32[]{:S(2)}) collective-permute-start(bf16[3,1,768,512]{3,2,1,0:T(8,128)(2,1)} %pad_maximum_fusion.2), channel_id=1, source_target_pairs={{1,0},{2,1},{3,2},{4,3},{5,4},{6,5},{7,6},{8,7},{9,8},{10,9},{11,1... | collective-permute-start | bytes 7077896 | tf_op jit(solution)/shard_map/ppermute | solution.py:18
  284.4 5.9 %copy-start = (bf16[1,1,768,256]{3,2,1,0:T(8,128)(2,1)S(1)}, bf16[1,1,768,256]{3,2,1,0:T(8,128)(2,1)}, u32[]{:S(2)}) copy-start(bf16[1,1,768,256]{3,2,1,0:T(8,128)(2,1)} %param.9) | copy-start | bytes 1179652
  284.4 5.9 %copy-start.1 = (s32[2,3]{1,0:T(2,128)S(1)}, s32[2,3]{1,0:T(2,128)}, u32[]{:S(2)}) copy-start(s32[2,3]{1,0:T(2,128)} %param.15) | copy-start | bytes 76
  297.3 5.3 %slice-start = ((s8[7077888]{0:T(1024)(128)(4,1)}), s8[4194304]{0:T(1024)(128)(4,1)S(1)}, s32[]{:S(2)}) async-start(s8[7077888]{0:T(1024)(128)(4,1)} %bitcast.37), calls=%async_computation | async-start | bytes 8388608 | tf_op jit(solution)/shard_map/while
  297.3 5.3 %slice-start.1 = ((s8[7077888]{0:T(1024)(128)(4,1)}), s8[2883584]{0:T(1024)(128)(4,1)S(1)}, s32[]{:S(2)}) async-start(s8[7077888]{0:T(1024)(128)(4,1)} %bitcast.37), calls=%async_computation.1 | async-start | bytes 5767168 | tf_op jit(solution)/shard_map/while
  317.9 5.3 %slice-start = ((s8[7077888]{0:T(1024)(128)(4,1)}), s8[4194304]{0:T(1024)(128)(4,1)S(1)}, s32[]{:S(2)}) async-start(s8[7077888]{0:T(1024)(128)(4,1)} %bitcast.37), calls=%async_computation | async-start | bytes 8388608 | tf_op jit(solution)/shard_map/while
  317.9 5.3 %slice-start.1 = ((s8[7077888]{0:T(1024)(128)(4,1)}), s8[2883584]{0:T(1024)(128)(4,1)S(1)}, s32[]{:S(2)}) async-start(s8[7077888]{0:T(1024)(128)(4,1)} %bitcast.37), calls=%async_computation.1 | async-start | bytes 5767168 | tf_op jit(solution)/shard_map/while
  331.6 0.7 copy-start.2
where the time goes:
time: 333 us; the launch traced here: 332 us
  blocking collectives  256 us (77%)
  other arithmetic  26.5 us (8%)
  matrix products  19.8 us (6%)
  starting transfers between devices  14.3 us (4%)
  waiting for transfers between devices  9.49 us (3%)
  local copies, waits for them, and re-layouts  5.73 us (2%)
    all_gather x1, blocking collectives, shards(): lax.all_gather(text_k, 'height', axis=0, tiled=True)  180 us
    all_gather x1, blocking collectives, shards(): lax.all_gather(text_v, 'height', axis=0, tiled=True)  76.3 us
    dot_general x4, matrix products, one_block(): jnp.einsum('qd,kd->qk', query_head, slab_all[:, low:high], preferred_elem...  9.85 us
    ppermute x2, starting transfers between devices, padded_2(): before = lax.ppermute(last, axis, up)  9.4 us
    dot_general x4, matrix products, one_block(): jnp.dot(video_expo.astype(jnp.bfloat16), slab_all[:, value_low:value_low...  7.99 us
    ppermute x2, waiting for transfers between devices, padded_2(): before = lax.ppermute(last, axis, up)  7.73 us
    concatenate x2, other arithmetic, padded_2(): array = jnp.concatenate([before, array, after], axis=dim)  7.55 us
    reduce_sum x8, other arithmetic, one_block(): row_total = jnp.sum(video_expo, axis=1) + jnp.sum(text_expo, axis=1)  6.88 us
  transfers between devices with their start and end apart: 4, of which 2 were waited for; matrix products, arithmetic and copies ran while one was open for 0% of the time, Pallas kernels for 0%

commit v1 on v0

--- a/solution.py
+++ b/solution.py
@@ -31,7 +31,9 @@
     padded = padded_2(key_value, (("tm", 0), ("height", 1)), 1)
     slab_all = padded.reshape(9 * row_count, 2 * feat_count)
     text_keys, text_values = (
-        lax.all_gather(text_k, "height", axis=0, tiled=True),
+        jnp.concatenate(
+            lax.all_to_all(jnp.stack(lax.axis_size("height") * [text_k], 0), "height", 0, 0), 0
+        ),
         lax.all_gather(text_v, "height", axis=0, tiled=True),
     )
     time_count = lax.axis_size("tm")

time: 333 us -> 261 us (0.78)
  the two profiles are of different devices: /device:TPU:4 before, /device:TPU:68 now
where the time goes in v1:
time: 261 us
  blocking collectives  169 us (65%)
  starting transfers between devices  28.5 us (11%)
  other arithmetic  26.5 us (10%)
  matrix products  19.8 us (8%)
  waiting for transfers between devices  9.49 us (4%)
  local copies, waits for them, and re-layouts  7.14 us (3%)
    all_gather x1, blocking collectives, shards(): lax.all_gather(text_v, 'height', axis=0, tiled=True)  169 us
    all_to_all x1, starting transfers between devices, shards(): lax.all_to_all(jnp.stack(lax.axis_size('height') * [text_k], 0), 'height'...  14.2 us
    dot_general x4, matrix products, one_block(): jnp.einsum('qd,kd->qk', query_head, slab_all[:, low:high], preferred_elem...  9.85 us
    ppermute x2, starting transfers between devices, padded_2(): before = lax.ppermute(last, axis, up)  9.4 us
    dot_general x4, matrix products, one_block(): jnp.dot(video_expo.astype(jnp.bfloat16), slab_all[:, value_low:value_low...  7.99 us
    ppermute x2, waiting for transfers between devices, padded_2(): before = lax.ppermute(last, axis, up)  7.73 us
    concatenate x2, other arithmetic, padded_2(): array = jnp.concatenate([before, array, after], axis=dim)  7.55 us
    reduce_sum x8, other arithmetic, one_block(): row_total = jnp.sum(video_expo, axis=1) + jnp.sum(text_expo, axis=1)  6.88 us
  transfers between devices with their start and end apart: 5, of which 2 were waited for; matrix products, arithmetic and copies ran while one was open for 3% of the time, Pallas kernels for 0%

profile of v1, /device:TPU:68, one launch (start us, length us, event | category | flops | bytes accessed | tf_op | source)
XLA Modules:
  0.0 260.6 jit_solution(3654370352824856805)
XLA Ops:
  0.0 1.0 constant_dynamic-update-slice_fusion.2
  1.0 1.0 constant_dynamic-update-slice_fusion.1
  2.1 1.9 collective-permute-start
  4.0 3.6 %collective-permute-start.1 = (bf16[1,1,768,512]{3,2,1,0:T(8,128)(2,1)S(1)}, bf16[1,1,768,512]{3,2,1,0:T(8,128)(2,1)S(1)}, u32[]{:S(2)}, u32[]{:S(2)}) collective-permute-start(bf16[1,1,768,512]{3,2,1,0:T(8,128)(2,1)S(1)} %constant_dynamic-update-slice_fusion.1), channel_id=1, source_target_pairs={{32,0},{64,32},{96,64},{128,96},{160,128},{192,160},{224,192},{256... | collective-permute-start | bytes 2359304 | tf_op jit(solution)/shard_map/ppermute | solution.py:18
  7.6 7.7 %collective-permute-done = bf16[1,1,768,512]{3,2,1,0:T(8,128)(2,1)S(1)} collective-permute-done((bf16[1,1,768,512]{3,2,1,0:T(8,128)(2,1)S(1)}, bf16[1,1,768,512]{3,2,1,0:T(8,128)(2,1)S(1)}, u32[]{:S(2)}, u32[]{:S(2)}) %collective-permute-start) | collective-permute-done | bytes 786464 | tf_op jit(solution)/shard_map/ppermute | solution.py:17
  15.4 1.8 collective-permute-done.1
  17.1 1.7 pad_maximum_fusion.2
  18.8 7.5 %collective-permute-start.2 = (bf16[3,1,768,512]{3,2,1,0:T(8,128)(2,1)}, bf16[3,1,768,512]{3,2,1,0:T(8,128)(2,1)}, u32[]{:S(2)}, u32[]{:S(2)}) collective-permute-start(bf16[3,1,768,512]{3,2,1,0:T(8,128)(2,1)} %pad_maximum_fusion.2), channel_id=1, source_target_pairs={{0,1},{1,2},{2,3},{3,4},{4,5},{5,6},{6,7},{7,8},{8,9},{9,10},{10,1... | collective-permute-start | bytes 7077896 | tf_op jit(solution)/shard_map/ppermute | solution.py:17
  26.3 1.3 collective-permute-start.3
  27.6 1.4 stack.2
  28.9 14.2 %all-to-all-start = ((bf16[32,8,256]{2,1,0:T(8,128)(2,1)}), bf16[32,8,256]{2,1,0:T(8,128)(2,1)S(1)}, u32[]{:S(2)}, u32[]{:S(2)}) async-start(bf16[32,8,256]{2,1,0:T(8,128)(2,1)} %stack.2), calls=%async_computation | async-start | bytes 262144 | tf_op jit(solution)/shard_map/all_to_all | solution.py:35
  43.2 168.8 %all_gather.3 = bf16[256,256]{1,0:T(8,128)(2,1)S(1)} all-gather(bf16[8,256]{1,0:T(8,128)(2,1)} %param.13), channel_id=1, replica_groups=mesh['tm'=16,'height'=32] {'height'}, dimensions={0}, use_global_device_ids=true | all-gather | bytes 135168 | tf_op jit(solution)/shard_map/all_gather | solution.py:37
  211.9 0.7 broadcast_compare_fusion
  212.6 5.9 %pad_maximum_fusion.1 = bf16[3,3,768,512]{3,2,1,0:T(8,128)(2,1)} fusion(bf16[3,1,768,512]{3,2,1,0:T(8,128)(2,1)} %collective-permute-done.3, bf16[1,1,768,512]{3,2,1,0:T(8,128)(2,1)S(1)} %collective-permute-done.1, bf16[1,1,768,512]{3,2,1,0:T(8,128)(2,1)S(1)} %constant_dynamic-update-slice_fusion.1, bf16[1,1,768,512]{3,2,1,0:T(8,128)(2,1)S(1)} %collective-permute-done, ...), kind=kLoop, calls=%fused_computation.95 | loop fusion | flops 14155776 | bytes 14155776 | tf_op jit(solution)/shard_map/concatenate | solution.py:19
  218.5 41.3 %while.15 = (s32[]{:T(128)}, bf16[2,384,256]{2,1,0:T(8,128)(2,1)S(1)}, s32[2,3]{1,0:T(2,128)S(1)}, s32[2]{0:T(128)S(1)}, bf16[2,384,256]{2,1,0:T(8,128)(2,1)S(1)...) while((s32[]{:T(128)}, ...), condition=%wide.region_9.10_spmd.clone.clone, body=%wide.region_0.9_spmd.clone.clone.sunk | while | flops 2858657792 | bytes 97717000 | solution.py:107
  218.6 0.7 fusion.102
  219.2 0.9 compare_reduce_fusion.10
  220.2 1.0 compare_reduce_fusion.11
  221.2 0.9 compare_reduce_fusion.8
  222.0 0.9 compare_reduce_fusion.9
  222.9 0.6 dynamic_slice.22
  223.5 2.0 compare_and_fusion.4
  225.5 3.3 %fusion.109 = (f32[384]{0:T(512)S(1)}, f32[384,6912]{1,0:T(8,128)S(1)}) fusion(bf16[6912,512]{1,0:T(8,128)(2,1)} %get-tuple-element.428, bf16[384,256]{1,0:T(8,128)(2,1)S(1)} %dynamic-slice_bitcast_fusion.2, pred[6912]{0:T(1024)(128)(4,1)S(1)} %get-tuple-element.394), kind=kOutput, calls=%fused_computation.103.clone.1 | convolution fusion | flops 687439488 | bytes 12493312 | tf_op jit(solution)/shard_map/while/body/eval_jaxpr/qd,kd->qk/dot_general | solution.py:70
  228.8 0.2 fusion.110
  229.1 1.6 fusion.112
  230.8 2.0 fusion.111
  232.8 0.2 fusion.114
  233.1 1.7 fusion.103
  234.7 0.2 fusion.104
  235.1 1.6 fusion.106
  236.7 2.0 fusion.105
  239.2 0.7 fusion.102
  239.9 0.9 compare_reduce_fusion.10
  240.8 1.0 compare_reduce_fusion.11
  241.8 0.9 compare_reduce_fusion.8
  242.7 0.9 compare_reduce_fusion.9
  243.5 0.6 dynamic_slice.22
  244.1 2.0 compare_and_fusion.4
  246.2 3.3 %fusion.109 = (f32[384]{0:T(512)S(1)}, f32[384,6912]{1,0:T(8,128)S(1)}) fusion(bf16[6912,512]{1,0:T(8,128)(2,1)} %get-tuple-element.428, bf16[384,256]{1,0:T(8,128)(2,1)S(1)} %dynamic-slice_bitcast_fusion.2, pred[6912]{0:T(1024)(128)(4,1)S(1)} %get-tuple-element.394), kind=kOutput, calls=%fused_computation.103.clone.1 | convolution fusion | flops 687439488 | bytes 12493312 | tf_op jit(solution)/shard_map/while/body/eval_jaxpr/qd,kd->qk/dot_general | solution.py:70
  249.4 0.2 fusion.110
  249.7 1.6 fusion.112
  251.5 2.0 fusion.111
  253.5 0.2 fusion.114
  253.7 1.7 fusion.103
  255.4 0.2 fusion.104
  255.7 1.6 fusion.106
  257.4 2.0 fusion.105
  259.8 0.7 copy-done.2
  (42 shorter events, 1.4 us)
Async XLA Ops:
  2.1 13.3 %collective-permute-start = (bf16[1,1,768,512]{3,2,1,0:T(8,128)(2,1)S(1)}, bf16[1,1,768,512]{3,2,1,0:T(8,128)(2,1)S(1)}, u32[]{:S(2)}, u32[]{:S(2)}) collective-permute-start(bf16[1,1,768,512]{3,2,1,0:T(8,128)(2,1)S(1)} %constant_dynamic-update-slice_fusion.1), channel_id=1, source_target_pairs={{0,32},{32,64},{64,96},{96,128},{128,160},{160,192},{192,224},{224... | collective-permute-start | bytes 2359304 | tf_op jit(solution)/shard_map/ppermute | solution.py:17
  4.0 13.1 %collective-permute-start.1 = (bf16[1,1,768,512]{3,2,1,0:T(8,128)(2,1)S(1)}, bf16[1,1,768,512]{3,2,1,0:T(8,128)(2,1)S(1)}, u32[]{:S(2)}, u32[]{:S(2)}) collective-permute-start(bf16[1,1,768,512]{3,2,1,0:T(8,128)(2,1)S(1)} %constant_dynamic-update-slice_fusion.1), channel_id=1, source_target_pairs={{32,0},{64,32},{96,64},{128,96},{160,128},{192,160},{224,192},{256... | collective-permute-start | bytes 2359304 | tf_op jit(solution)/shard_map/ppermute | solution.py:18
  18.8 193.8 %collective-permute-start.2 = (bf16[3,1,768,512]{3,2,1,0:T(8,128)(2,1)}, bf16[3,1,768,512]{3,2,1,0:T(8,128)(2,1)}, u32[]{:S(2)}, u32[]{:S(2)}) collective-permute-start(bf16[3,1,768,512]{3,2,1,0:T(8,128)(2,1)} %pad_maximum_fusion.2), channel_id=1, source_target_pairs={{0,1},{1,2},{2,3},{3,4},{4,5},{5,6},{6,7},{7,8},{8,9},{9,10},{10,1... | collective-permute-start | bytes 7077896 | tf_op jit(solution)/shard_map/ppermute | solution.py:17
  26.3 186.4 %collective-permute-start.3 = (bf16[3,1,768,512]{3,2,1,0:T(8,128)(2,1)}, bf16[3,1,768,512]{3,2,1,0:T(8,128)(2,1)}, u32[]{:S(2)}, u32[]{:S(2)}) collective-permute-start(bf16[3,1,768,512]{3,2,1,0:T(8,128)(2,1)} %pad_maximum_fusion.2), channel_id=1, source_target_pairs={{1,0},{2,1},{3,2},{4,3},{5,4},{6,5},{7,6},{8,7},{9,8},{10,9},{11,1... | collective-permute-start | bytes 7077896 | tf_op jit(solution)/shard_map/ppermute | solution.py:18
  28.9 189.6 %all-to-all-start = ((bf16[32,8,256]{2,1,0:T(8,128)(2,1)}), bf16[32,8,256]{2,1,0:T(8,128)(2,1)S(1)}, u32[]{:S(2)}, u32[]{:S(2)}) async-start(bf16[32,8,256]{2,1,0:T(8,128)(2,1)} %stack.2), calls=%async_computation | async-start | bytes 262144 | tf_op jit(solution)/shard_map/all_to_all | solution.py:35
  212.6 5.9 %copy-start = (bf16[1,1,768,256]{3,2,1,0:T(8,128)(2,1)S(1)}, bf16[1,1,768,256]{3,2,1,0:T(8,128)(2,1)}, u32[]{:S(2)}) copy-start(bf16[1,1,768,256]{3,2,1,0:T(8,128)(2,1)} %param.9) | copy-start | bytes 1179652
  212.6 5.9 %copy-start.1 = (s32[2,3]{1,0:T(2,128)S(1)}, s32[2,3]{1,0:T(2,128)}, u32[]{:S(2)}) copy-start(s32[2,3]{1,0:T(2,128)} %param.15) | copy-start | bytes 76
  225.5 5.3 %slice-start = ((s8[7077888]{0:T(1024)(128)(4,1)}), s8[4194304]{0:T(1024)(128)(4,1)S(1)}, s32[]{:S(2)}) async-start(s8[7077888]{0:T(1024)(128)(4,1)} %bitcast.38), calls=%async_computation.1 | async-start | bytes 8388608 | tf_op jit(solution)/shard_map/while
  225.5 5.3 %slice-start.1 = ((s8[7077888]{0:T(1024)(128)(4,1)}), s8[2883584]{0:T(1024)(128)(4,1)S(1)}, s32[]{:S(2)}) async-start(s8[7077888]{0:T(1024)(128)(4,1)} %bitcast.38), calls=%async_computation.2 | async-start | bytes 5767168 | tf_op jit(solution)/shard_map/while
  246.2 5.3 %slice-start = ((s8[7077888]{0:T(1024)(128)(4,1)}), s8[4194304]{0:T(1024)(128)(4,1)S(1)}, s32[]{:S(2)}) async-start(s8[7077888]{0:T(1024)(128)(4,1)} %bitcast.38), calls=%async_computation.1 | async-start | bytes 8388608 | tf_op jit(solution)/shard_map/while
  246.2 5.3 %slice-start.1 = ((s8[7077888]{0:T(1024)(128)(4,1)}), s8[2883584]{0:T(1024)(128)(4,1)S(1)}, s32[]{:S(2)}) async-start(s8[7077888]{0:T(1024)(128)(4,1)} %bitcast.38), calls=%async_computation.2 | async-start | bytes 5767168 | tf_op jit(solution)/shard_map/while
  259.8 0.7 copy-start.2
